TPU v7x, 256 devices: a whole 4x4x8 slice. The times are simulated.
256 devices in a mesh: pair: 32 (over x, y, core), slab: 8 (over z).
Axes of the slice: x: 4, y: 4, z: 8, core: 2. Of those that a mesh axis runs over, the one named last changes fastest.
Arguments:
- amplitudes: bfloat16 [6144, 9216], P('pair', 'slab'), may hold values from -6 to 6
- integrals: bfloat16 [9216, 9216], P('slab', 'pair'), may hold values from -0.125 to 0.125
- pair_index: int32 [6144, 2], P('pair'), may hold values from 0 to 159, as said below
- eps_occ: float32 [160], replicated, may hold values from -2 to -0.5
- eps_vir: float32 [96], replicated, may hold values from 0.5 to 3
Outputs:
- update: float32 [6144, 9216], P('pair', 'slab')
Inputs may be any that keep to these rules, and one draw needn't show every extreme that they name: `pair_index`: each row holds i < j; pairs may repeat; pair 0 is (0, 159).
All inputs are finite; a program needn't handle non-finite values.
Results may differ from a plain program's by a relative error of at most 0.0003.
Values may be sent and summed in bfloat16 or wider, within the bound.
A program may use at most 128 MiB of HBM per device.

v0:
```python
import functools

import jax
import jax.numpy as jnp
import numpy as np
from jax import lax
from jax.experimental import pallas as pl
from jax.experimental.pallas import tpu as pltpu
from jax.sharding import PartitionSpec as P

MESH = pl.DeviceIdType.MESH
G = 12
ROWS = 40
HALF = 72
QMAX = 32767.0


def selection_tables():
    sel = np.zeros((3, 2, HALF, 4 * ROWS), np.float32)
    for kind in range(3):
        for i in range(6):
            for v in range(G):
                u, vv = i, v
                if kind == 1:
                    u = i + 6
                if kind == 2 and v < i:
                    u, vv = i + 6, v + 6
                sel[kind, 0, i * G + v, ROWS * (u // 3) + G * (u % 3) + vv] = 1
                sel[kind, 1, i * G + v, ROWS * (vv // 3) + G * (vv % 3) + u] = 1
    return sel


def output_tables():
    table = np.zeros((8, 4, G * 8 * G), np.int32)
    for w in range(8):
        for a in range(G):
            for o in range(8):
                for b in range(G):
                    col = (a * 8 + o) * G + b
                    if o > w:
                        u, v, s, h = a, b, 1, a // 6
                    elif o < w:
                        u, v, s, h = b, a, -1, b // 6
                    else:
                        lo, hi, s, h = min(a, b), max(a, b), (0 if a == b else 1 if a < b else -1), 0
                        if lo >= 6:
                            u, v, s = hi - 6, lo - 6, -s
                        else:
                            u, v = lo, hi
                    table[w, :, col] = (o * 2 + h) * HALF + (u % 6) * G + v, w * G + a, o * G + b, s
    return table


def row_order():
    order = np.zeros((8 * ROWS, 3 * 8 * G), np.float32)
    for o in range(8):
        for a in range(3):
            for b in range(G):
                order[o * ROWS + a * G + b, (a * 8 + o) * G + b] = 1
    return order


def xor3(a, b):
    out = 0
    for bit in (1, 2, 4):
        out = out + bit * lax.rem(lax.div(a, bit) + lax.div(b, bit), 2)
    return out


def quantize(val, q_ref, s_ref):
    n, r, width = val.shape
    cube = val.reshape(n * r // 8, 8, width)
    top = jnp.maximum(jnp.max(jnp.abs(cube), axis=0) * (1.01 / QMAX), 1e-36).astype(jnp.bfloat16)
    q = (cube * (1.0 / top.astype(jnp.float32)) + 32768.5).astype(jnp.int32) - 32768
    q_ref[...] = q.reshape(n, r, width).astype(jnp.int16)
    s_ref[...] = top


def dequantize(q, s):
    n, r, width = q.shape
    cube = q.astype(jnp.int32).astype(jnp.float32).reshape(n * r // 8, 8, width)
    return (cube * s.astype(jnp.float32)).reshape(n, r, width)


def column(row):
    n = row.shape[1]
    same = lax.broadcasted_iota(jnp.int32, (n, n), 0) == lax.broadcasted_iota(jnp.int32, (n, n), 1)
    return jnp.sum(jnp.where(same, row, 0.0), axis=1, keepdims=True)


def looked_up(ids, table):
    hit = lax.broadcasted_iota(jnp.int32, (table.shape[0], ids.shape[1]), 0) == ids
    return jnp.sum(jnp.where(hit, table, 0.0), axis=0, keepdims=True)


def kernel(sel_ref, order_ref, table_ref, a_ref, vt_ref, pairs_ref, occ_ref, vir_ref, out_ref,
           a_all, v_ref, v_buf, v1, v2, cs, rq, rs, sq, ss, fq, fs, gq, gs, w_ref, o_ref, ep_ref, ev_ref,
           vx_s, vx_r, vy_s, vy_r, vf_s, vf_r, ax_s, ax_r, af_s, af_r, ap_s, ap_r, own_s,
           rq_s, rq_r, rs_s, rs_r, fq_s, fq_r, fs_s, fs_r):
    pair, z = lax.axis_index("pair"), lax.axis_index("slab")
    x, y, c = lax.div(pair, 8), lax.rem(lax.div(pair, 2), 4), lax.rem(pair, 2)

    def kid(xx, cc):
        return xx + 4 * cc

    kappa = kid(x, c)
    w_mine = lax.div(pair, 4)

    def dev(xx, yy, cc, zz):
        return ((xx * 4 + yy) * 2 + cc, zz)

    def step(i, d, n):
        return lax.rem(i + d + n, n)

    def remote(src, dst, ssem, rsem, to):
        return pltpu.make_async_remote_copy(
            src_ref=src, dst_ref=dst, send_sem=ssem, recv_sem=rsem, device_id=to, device_id_type=MESH
        )

    barrier = pltpu.get_barrier_semaphore()

    def greet(to):
        pl.semaphore_signal(barrier, inc=1, device_id=to, device_id_type=MESH)

    for dx in range(4):
        for dc in range(2):
            if dx or dc:
                greet(dev(step(x, dx, 4), y, step(c, dc, 2), z))
    for d in (1, -1):
        greet(dev(x, step(y, d, 4), c, z))
        greet(dev(x, y, c, step(z, d, 8)))
    ordered = jnp.dot(order_ref[...], vt_ref[...], preferred_element_type=jnp.float32).astype(jnp.bfloat16)
    v_ref[...] = ordered.reshape(v_ref.shape)
    pl.semaphore_wait(barrier, 11)

    slot_y = lax.rem(y, 2) * 2
    copies = []
    for dx in (1, 3, 2, 0):
        for dc in (0, 1):
            xx, cc = step(x, dx, 4), step(c, dc, 2)
            k = kid(xx, cc)
            src = v_ref.at[xor3(w_mine, k)]
            dst = v_buf.at[w_mine, slot_y + c]
            if dx or dc:
                cp = remote(src, dst, vx_s.at[dx * 2 + dc], vx_r.at[kappa], dev(xx, y, cc, z))
            else:
                cp = pltpu.make_async_copy(src, dst, own_s.at[0])
            cp.start()
            copies.append((dx or dc, cp))
    for d, di in ((1, 0), (-1, 1)):
        for h in range(2):
            part = pl.ds(96 * h, 96)
            remote(a_ref.at[part], a_all.at[x, c, part], ax_s.at[di, h], ax_r.at[di, h], dev(step(x, d, 4), y, c, z)).start()
    other = dev(x, y, 1 - c, z)
    remote(a_ref, a_all.at[x, c], ap_s.at[0], ap_r.at[0], other).start()
    own_a = pltpu.make_async_copy(a_ref, a_all.at[x, c], own_s.at[1])
    own_a.start()

    def v_slot(yy, xx, cc):
        return v_buf.at[2 * xx + lax.div(yy, 2), lax.rem(yy, 2) * 2 + cc]

    def to_y(d):
        return dev(x, step(y, d, 4), c, z)

    for dx in (0, 1, 3, 2):
        for dc in range(2):
            xx, cc = step(x, dx, 4), step(c, dc, 2)
            blk = v_slot(y, xx, cc)
            if dx or dc:
                remote(blk, blk, vx_s.at[0], vx_r.at[kid(xx, cc)], other).wait_recv()
            else:
                copies[-2][1].wait()
            for d, di in ((1, 0), (-1, 1)):
                u = dx * 2 + cc
                remote(blk, blk, vy_s.at[di, u], vy_r.at[di, u], to_y(d)).start()

    for d, di in ((1, 0), (-1, 1)):
        blk = a_all.at[step(x, -d, 4), c, pl.ds(96 * di, 96)]
        remote(blk, blk, ax_s.at[di, di], ax_r.at[di, di], other).wait_recv()
        remote(blk, blk, af_s.at[di], af_r.at[di], dev(step(x, d, 4), y, c, z)).start()

    table = table_ref[z]
    sign = table[3:4].astype(jnp.float32)

    @pl.loop(0, 9)
    def _(i):
        rows = lax.broadcasted_iota(jnp.int32, (128, 8 * G * G), 0) + i * 128
        hit = rows == table[0:1]
        w_ref[pl.ds(pl.multiple_of(i * 128, 128), 128), :] = jnp.where(hit, sign, 0.0).astype(jnp.bfloat16)

    vir, occ = column(vir_ref[...]), column(occ_ref[...])
    ev_ref[...] = looked_up(table[1:2], vir) + looked_up(table[2:3], vir)
    ep_ref[...] = column(looked_up(pairs_ref[0:1], occ) + looked_up(pairs_ref[1:2], occ))

    for dx in (0, 1, 3, 2):
        for d, di in ((1, 0), (-1, 1)):
            u = dx * 2 + di
            blk = v_slot(step(y, -d, 4), step(x, dx, 4), di)
            remote(blk, blk, vy_s.at[di, u], vy_r.at[di, u], other).wait_recv()
            remote(blk, blk, vf_s.at[u], vf_r.at[u], to_y(d)).start()

    for n, d, di in ((1, 1, 0), (2, -1, 1)):
        blk = a_all.at[step(x, -d, 4), c]
        part = a_all.at[step(x, -d, 4), c, pl.ds(96 * (1 - di), 96)]
        remote(part, part, ax_s.at[di, 1 - di], ax_r.at[di, 1 - di], other).wait_recv()
        remote(blk, blk, ap_s.at[n], ap_r.at[n], other).start()
    far = a_all.at[step(x, 2, 4), c]
    for di in range(2):
        part = a_all.at[step(x, 2, 4), c, pl.ds(96 * di, 96)]
        remote(part, part, af_s.at[di], af_r.at[di], other).wait_recv()
    remote(far, far, ap_s.at[3], ap_r.at[3], other).start()

    for d, di in ((1, 0), (-1, 1)):
        for dx in (0, 1, 3, 2):
            u = dx * 2 + 1 - di
            blk = v_slot(step(y, -d, 4), step(x, dx, 4), 1 - di)
            remote(blk, blk, vy_s.at[di, u], vy_r.at[di, u], other).wait_recv()
    for dx in (0, 1, 3, 2):
        for di in range(2):
            u = dx * 2 + di
            blk = v_slot(step(y, 2, 4), step(x, dx, 4), di)
            remote(blk, blk, vf_s.at[u], vf_r.at[u], other).wait_recv()

    targets = (4, 3, -3, 2, -2, 1, -1, 0)

    def select(j):
        t = step(z, targets[j], 8)
        o = xor3(t, kappa)
        lo, hi = jnp.minimum(t, o), jnp.maximum(t, o)
        kind = jnp.where(kappa == 0, 2, jnp.where(t == lo, 0, 1))
        rows = pl.ds(j * HALF, HALF)
        v1[rows, :] = jnp.dot(
            sel_ref[kind, 0], v_buf[lo].reshape(4 * ROWS, -1), preferred_element_type=jnp.float32
        ).astype(jnp.bfloat16)
        v2[rows, :] = jnp.dot(
            sel_ref[kind, 1], v_buf[hi].reshape(4 * ROWS, -1), preferred_element_type=jnp.float32
        ).astype(jnp.bfloat16)

    nt = (((1,), (1,)), ((), ()))

    def products(first, last):
        rows = pl.ds(first * HALF, (last - first) * HALF)

        @pl.loop(0, 4)
        def _(i):
            rows_a = a_all[i].reshape(2 * a_all.shape[2], -1)
            cs[i, rows] = lax.dot_general(
                v1[rows, :], rows_a, nt, preferred_element_type=jnp.float32
            ) - lax.dot_general(v2[rows, :], rows_a, nt, preferred_element_type=jnp.float32)

    for j in range(3):
        select(j)
    own_a.wait()
    for n, dx in ((0, 0), (1, -1), (2, 1), (3, 2)):
        blk = a_all.at[step(x, dx, 4), 1 - c]
        remote(blk, blk, ap_s.at[n], ap_r.at[n], other).wait_recv()

    products(0, 3)

    def chunk(t, h):
        j = targets.index(4 if t == -4 else t)
        return cs[pl.ds(2 * h, 2), pl.ds(j * HALF, HALF), :]

    streams = [(1, 0, 3), (-1, 0, 4), (1, 1, 4), (-1, 1, 3)]

    def hop(i, s, d):
        to = dev(x, y, c, step(z, d, 8))
        return (
            remote(sq.at[i, s], rq.at[i, s], rq_s.at[i, s], rq_r.at[i, s], to),
            remote(ss.at[i, s], rs.at[i, s], rs_s.at[i, s], rs_r.at[i, s], to),
        )

    for s in range(4):
        for i, (d, h, length) in enumerate(streams):
            if s >= length:
                continue
            val = chunk(d * (length - s), h)
            if s:
                for cp in hop(i, s - 1, d):
                    cp.wait_recv()
                val = val + dequantize(rq[i, s - 1], rs[i, s - 1])
            quantize(val, sq.at[i, s], ss.at[i, s])
            for cp in hop(i, s, d):
                cp.start()
        if s == 0:
            for j in range(3, 8):
                select(j)
            products(3, 8)

    gq[2 * z + 1] = jnp.zeros(gq.shape[1:], gq.dtype)
    gs[2 * z + 1] = jnp.zeros(gs.shape[1:], gs.dtype)
    for h in range(2):
        val = chunk(0, h)
        for i, (d, hh, length) in enumerate(streams):
            if hh == h:
                for cp in hop(i, length - 1, d):
                    cp.wait_recv()
                val = val + dequantize(rq[i, length - 1], rs[i, length - 1])
        for i in range(2):
            quantize(val[i : i + 1], fq.at[pl.ds(2 * h + i, 1)], fs.at[2 * h + i])

    o = xor3(z, kappa)
    end = jnp.where(z > o, 1, 0)

    def deliver(dx, dc, mirror):
        xx, cc = step(x, dx, 4), step(c, dc, 2)
        lanes = pl.ds(pl.multiple_of(128 * cc, 128), 256)
        slot = 2 * (z if mirror else o) + end
        n, m = (dx * 2 + dc), int(mirror)
        to = dev(xx, y, cc, o if mirror else z)
        if not (dx or dc or mirror):
            return (
                pltpu.make_async_copy(fq.at[xx, :, lanes], gq.at[slot], own_s.at[2]),
                pltpu.make_async_copy(fs.at[xx, :, lanes], gs.at[slot], own_s.at[3]),
            )
        return (
            remote(fq.at[xx, :, lanes], gq.at[slot], fq_s.at[m, n], fq_r.at[m, kappa], to),
            remote(fs.at[xx, :, lanes], gs.at[slot], fs_s.at[m, n], fs_r.at[m, kappa], to),
        )

    order = [(dx, dc) for dx in (2, 1, 3, 0) for dc in (0, 1)]

    @pl.when(kappa > 0)
    def _():
        for dx, dc in order:
            for cp in deliver(dx, dc, True):
                cp.start()

    for dx, dc in order:
        for cp in deliver(dx, dc, False):
            cp.start()

    def arrived(m, k):
        remote(fq.at[0, :, pl.ds(0, 256)], gq.at[0], fq_s.at[0, 0], fq_r.at[m, k], other).wait_recv()
        remote(fs.at[0, :, pl.ds(0, 256)], gs.at[0], fs_s.at[0, 0], fs_r.at[m, k], other).wait_recv()

    tn = (((0,), (0,)), ((), ()))
    for n, (dx, dc) in enumerate(((0, 0), (0, 1), (1, 0), (1, 1), (3, 0), (3, 1), (2, 0), (2, 1))):
        k = kid(step(x, dx, 4), step(c, dc, 2))
        if dx or dc:
            arrived(0, k)
        else:
            for cp in deliver(0, 0, False):
                cp.wait()

        @pl.when(k > 0)
        def _():
            arrived(1, k)

        o = xor3(z, k)
        full = jnp.concatenate(
            [dequantize(gq[pl.ds(2 * o + i, 1)], gs[2 * o + i])[0] for i in range(2)], axis=0
        )
        top = full.astype(jnp.bfloat16)
        low = (full - top.astype(jnp.float32)).astype(jnp.bfloat16)
        w_rows = w_ref[pl.ds(pl.multiple_of(o * 2 * HALF, 16), 2 * HALF), :]
        part = lax.dot_general(top, w_rows, tn, preferred_element_type=jnp.float32) + lax.dot_general(
            low, w_rows, tn, preferred_element_type=jnp.float32
        )
        o_ref[...] = part if n == 0 else o_ref[...] + part
    out_ref[...] = o_ref[pl.ds(pl.multiple_of(64 * c, 8), out_ref.shape[0]), :] / (ep_ref[...] - ev_ref[...])

    for dx in range(4):
        for dc in range(2):
            n = dx * 2 + dc
            if n:
                remote(v_ref.at[0], v_buf.at[0, 0], vx_s.at[n], vx_r.at[0], other).wait_send()
            for di in range(2):
                remote(v_ref.at[0], v_buf.at[0, 0], vy_s.at[di, n], vx_r.at[0], other).wait_send()
            remote(v_ref.at[0], v_buf.at[0, 0], vf_s.at[n], vx_r.at[0], other).wait_send()
    half_a = a_ref.at[pl.ds(0, 96)]
    for di in range(2):
        for h in range(2):
            remote(half_a, half_a, ax_s.at[di, h], ax_r.at[di, h], other).wait_send()
        remote(half_a, half_a, af_s.at[di], af_r.at[di], other).wait_send()
    for n in range(4):
        remote(a_ref, a_ref, ap_s.at[n], ap_r.at[n], other).wait_send()
    for i, (d, h, length) in enumerate(streams):
        for s in range(length):
            for cp in hop(i, s, d):
                cp.wait_send()
    for dx, dc in order:
        if dx or dc:
            for cp in deliver(dx, dc, False):
                cp.wait_send()

    @pl.when(kappa > 0)
    def _():
        for dx, dc in order:
            for cp in deliver(dx, dc, True):
                cp.wait_send()


def on_device(amplitudes, integrals, pair_index, eps_occ, eps_vir):
    rows, depth = amplitudes.shape
    f32, bf16, i16 = jnp.float32, jnp.bfloat16, jnp.int16
    dma = pltpu.SemaphoreType.DMA
    return pl.pallas_call(
        kernel,
        out_shape=jax.ShapeDtypeStruct((rows, 8 * G * G), f32),
        in_specs=[pl.BlockSpec(memory_space=pltpu.VMEM)] * 8,
        out_specs=pl.BlockSpec(memory_space=pltpu.VMEM),
        scratch_shapes=[
            pltpu.VMEM((4, 2, rows, depth), bf16),
            pltpu.VMEM((8, ROWS, depth), bf16),
            pltpu.VMEM((8, 4, ROWS, depth), bf16),
            pltpu.VMEM((8 * HALF, depth), bf16),
            pltpu.VMEM((8 * HALF, depth), bf16),
            pltpu.VMEM((4, 8 * HALF, 2 * rows), f32),
            pltpu.VMEM((4, 4, 2, HALF, 2 * rows), i16),
            pltpu.VMEM((4, 4, 8, 2 * rows), bf16),
            pltpu.VMEM((4, 4, 2, HALF, 2 * rows), i16),
            pltpu.VMEM((4, 4, 8, 2 * rows), bf16),
            pltpu.VMEM((4, HALF, 2 * rows), i16),
            pltpu.VMEM((4, 8, 2 * rows), bf16),
            pltpu.VMEM((16, HALF, 256), i16),
            pltpu.VMEM((16, 8, 256), bf16),
            pltpu.VMEM((16 * HALF, 8 * G * G), bf16),
            pltpu.VMEM((256, 8 * G * G), f32),
            pltpu.VMEM((rows, 1), f32),
            pltpu.VMEM((1, 8 * G * G), f32),
            dma((8,)), dma((8,)), dma((2, 8)), dma((2, 8)), dma((8,)), dma((8,)),
            dma((2, 2)), dma((2, 2)), dma((2,)), dma((2,)), dma((4,)), dma((4,)), dma((4,)),
            dma((4, 4)), dma((4, 4)), dma((4, 4)), dma((4, 4)),
            dma((2, 8)), dma((2, 8)), dma((2, 8)), dma((2, 8)),
        ],
        compiler_params=pltpu.CompilerParams(
            collective_id=0, has_side_effects=True, vmem_limit_bytes=60 * 1024 * 1024
        ),
    )(
        jnp.asarray(selection_tables(), bf16),
        jnp.asarray(row_order(), bf16),
        jnp.asarray(output_tables()),
        amplitudes,
        integrals.T,
        pair_index.T,
        eps_occ.reshape(1, -1),
        eps_vir.reshape(1, -1),
    )


def solution(mesh):
    in_specs = (P("pair", "slab"), P("slab", "pair"), P("pair", None), P(), P())
    return jax.shard_map(on_device, mesh=mesh, in_specs=in_specs, out_specs=P("pair", "slab"), check_vma=False)
```

profile of v0, /device:TPU:1, one launch (start us, length us, event | category | flops | bytes accessed | tf_op | source)
XLA Modules:
  0.0 83.4 jit_solution(7145680349041785469)
XLA Ops:
  0.0 81.3 %shard_map.82 = f32[192,1152]{1,0:T(8,128)} custom-call(bf16[3,2,72,160]{3,2,1,0:T(8,128)(2,1)} %constant.6.clone.sel_ref, bf16[320,288]{1,0:T(8,128)(2,1)} %constant.7.clone.order_ref, s32[8,4,1152]{2,1,0:T(4,128)} %constant.8.clone.table_ref, bf16[192,1152]{1,0:T(8,128)(2,1)} %a_ref.1, bf16[288,1152]{1,0:T(8,128)(2,1)} %bitcast.4, s32[2,192]{1,0:T(2,128)} %bitcast.5, ...), custom_call_target="tpu_custom_call" | custom-call | tf_op jit(solution)/shard_map/pallas_call | solution.py:398
  81.3 2.1 %copy.10 = f32[192,1152]{1,0:T(8,128)} copy(f32[192,1152]{1,0:T(8,128)} %shard_map.82) | data formatting | bytes 1769472
where the time goes:
time: 83.8 us; the launch traced here: 83.4 us
  Pallas kernels  81.3 us (97%)
  local copies, waits for them, and re-layouts  2.14 us (3%)
    pallas_call x1, Pallas kernels, on_device(): pl.pallas_call(kernel, out_shape=jax.ShapeDtypeStruct((rows, 8 * G * G),...  81.3 us
    unnamed x1, local copies, waits for them, and re-layouts  2.14 us

commit v1 on v0

--- a/solution.py
+++ b/solution.py
@@ -68,18 +68,21 @@
 
 
 def quantize(val, q_ref, s_ref):
-    n, r, width = val.shape
-    cube = val.reshape(n * r // 8, 8, width)
-    top = jnp.maximum(jnp.max(jnp.abs(cube), axis=0) * (1.01 / QMAX), 1e-36).astype(jnp.bfloat16)
-    q = (cube * (1.0 / top.astype(jnp.float32)) + 32768.5).astype(jnp.int32) - 32768
-    q_ref[...] = q.reshape(n, r, width).astype(jnp.int16)
+    r, width = val.shape
+    cube = val.reshape(r // 8, 8, width)
+    top = jnp.max(jnp.abs(cube), axis=0)
+    top = functools.reduce(jnp.maximum, [top[:, 128 * i : 128 * (i + 1)] for i in range(width // 128)])
+    top = jnp.maximum(top * (1.01 / QMAX), 1e-36).astype(jnp.bfloat16)
+    inv = 1.0 / top.astype(jnp.float32)
+    q = (cube * jnp.concatenate([inv] * (width // 128), axis=1) + 32768.5).astype(jnp.int32) - 32768
+    q_ref[...] = q.reshape(r, width).astype(jnp.int16)
     s_ref[...] = top
 
 
 def dequantize(q, s):
-    n, r, width = q.shape
-    cube = q.astype(jnp.int32).astype(jnp.float32).reshape(n * r // 8, 8, width)
-    return (cube * s.astype(jnp.float32)).reshape(n, r, width)
+    r, width = q.shape
+    cube = q.astype(jnp.int32).astype(jnp.float32).reshape(r // 8, 8, width)
+    return (cube * jnp.concatenate([s.astype(jnp.float32)] * (width // 128), axis=1)).reshape(r, width)
 
 
 def column(row):
@@ -93,7 +96,8 @@
     return jnp.sum(jnp.where(hit, table, 0.0), axis=0, keepdims=True)
 
 
-def kernel(sel_ref, order_ref, table_ref, a_ref, vt_ref, pairs_ref, occ_ref, vir_ref, out_ref,
+def kernel(sel_hbm, order_hbm, table_hbm, a_hbm, vt_hbm, pairs_hbm, occ_hbm, vir_hbm, out_hbm,
+           sel_ref, order_ref, table_ref, vt_ref, pairs_ref, occ_ref, vir_ref, in_s, out_s, out_ref,
            a_all, v_ref, v_buf, v1, v2, cs, rq, rs, sq, ss, fq, fs, gq, gs, w_ref, o_ref, ep_ref, ev_ref,
            vx_s, vx_r, vy_s, vy_r, vf_s, vf_r, ax_s, ax_r, af_s, af_r, ap_s, ap_r, own_s,
            rq_s, rq_r, rs_s, rs_r, fq_s, fq_r, fs_s, fs_r):
@@ -116,6 +120,19 @@
         return pltpu.make_async_remote_copy(
             src_ref=src, dst_ref=dst, send_sem=ssem, recv_sem=rsem, device_id=to, device_id_type=MESH
         )
+
+    a_ref = a_all.at[x, c]
+    inputs = [
+        pltpu.make_async_copy(src, dst, in_s.at[i])
+        for i, (src, dst) in enumerate(
+            (
+                (order_hbm, order_ref), (vt_hbm, vt_ref), (a_hbm, a_ref), (table_hbm, table_ref), (sel_hbm, sel_ref),
+                (pairs_hbm, pairs_ref), (occ_hbm, occ_ref), (vir_hbm, vir_ref),
+            )
+        )
+    ]
+    for cp in inputs:
+        cp.start()
 
     barrier = pltpu.get_barrier_semaphore()
 
@@ -129,6 +146,8 @@
     for d in (1, -1):
         greet(dev(x, step(y, d, 4), c, z))
         greet(dev(x, y, c, step(z, d, 8)))
+    inputs[0].wait()
+    inputs[1].wait()
     ordered = jnp.dot(order_ref[...], vt_ref[...], preferred_element_type=jnp.float32).astype(jnp.bfloat16)
     v_ref[...] = ordered.reshape(v_ref.shape)
     pl.semaphore_wait(barrier, 11)
@@ -147,14 +166,13 @@
                 cp = pltpu.make_async_copy(src, dst, own_s.at[0])
             cp.start()
             copies.append((dx or dc, cp))
+    inputs[2].wait()
     for d, di in ((1, 0), (-1, 1)):
         for h in range(2):
-            part = pl.ds(96 * h, 96)
-            remote(a_ref.at[part], a_all.at[x, c, part], ax_s.at[di, h], ax_r.at[di, h], dev(step(x, d, 4), y, c, z)).start()
+            part = a_all.at[x, c, pl.ds(96 * h, 96)]
+            remote(part, part, ax_s.at[di, h], ax_r.at[di, h], dev(step(x, d, 4), y, c, z)).start()
     other = dev(x, y, 1 - c, z)
-    remote(a_ref, a_all.at[x, c], ap_s.at[0], ap_r.at[0], other).start()
-    own_a = pltpu.make_async_copy(a_ref, a_all.at[x, c], own_s.at[1])
-    own_a.start()
+    remote(a_ref, a_ref, ap_s.at[0], ap_r.at[0], other).start()
 
     def v_slot(yy, xx, cc):
         return v_buf.at[2 * xx + lax.div(yy, 2), lax.rem(yy, 2) * 2 + cc]
@@ -179,6 +197,8 @@
         remote(blk, blk, ax_s.at[di, di], ax_r.at[di, di], other).wait_recv()
         remote(blk, blk, af_s.at[di], af_r.at[di], dev(step(x, d, 4), y, c, z)).start()
 
+    for cp in inputs[3:]:
+        cp.wait()
     table = table_ref[z]
     sign = table[3:4].astype(jnp.float32)
 
@@ -238,104 +258,124 @@
 
     nt = (((1,), (1,)), ((), ()))
 
-    def products(first, last):
+    rel = (0, 1, 3, 2)
+
+    def products(groups, first, last):
         rows = pl.ds(first * HALF, (last - first) * HALF)
 
-        @pl.loop(0, 4)
-        def _(i):
-            rows_a = a_all[i].reshape(2 * a_all.shape[2], -1)
-            cs[i, rows] = lax.dot_general(
+        @pl.loop(groups[0], groups[1])
+        def _(g):
+            rows_a = a_all[step(x, jnp.where(g < 2, g, 5 - g), 4)].reshape(2 * a_all.shape[2], -1)
+            cs[g, rows] = lax.dot_general(
                 v1[rows, :], rows_a, nt, preferred_element_type=jnp.float32
             ) - lax.dot_general(v2[rows, :], rows_a, nt, preferred_element_type=jnp.float32)
 
     for j in range(3):
         select(j)
-    own_a.wait()
-    for n, dx in ((0, 0), (1, -1), (2, 1), (3, 2)):
+
+    def other_core(n, dx):
         blk = a_all.at[step(x, dx, 4), 1 - c]
         remote(blk, blk, ap_s.at[n], ap_r.at[n], other).wait_recv()
 
-    products(0, 3)
-
-    def chunk(t, h):
+    other_core(0, 0)
+    other_core(2, 1)
+    products((0, 2), 0, 3)
+
+    def chunk(t, g):
         j = targets.index(4 if t == -4 else t)
-        return cs[pl.ds(2 * h, 2), pl.ds(j * HALF, HALF), :]
-
-    streams = [(1, 0, 3), (-1, 0, 4), (1, 1, 4), (-1, 1, 3)]
-
-    def hop(i, s, d):
+        return cs[g, pl.ds(j * HALF, HALF), :]
+
+    def streams(g):
+        return ((1, 0, 3 + g % 2), (-1, 1, 4 - g % 2))
+
+    def hop(g, i, s, d):
         to = dev(x, y, c, step(z, d, 8))
         return (
-            remote(sq.at[i, s], rq.at[i, s], rq_s.at[i, s], rq_r.at[i, s], to),
-            remote(ss.at[i, s], rs.at[i, s], rs_s.at[i, s], rs_r.at[i, s], to),
-        )
-
-    for s in range(4):
-        for i, (d, h, length) in enumerate(streams):
-            if s >= length:
-                continue
-            val = chunk(d * (length - s), h)
-            if s:
-                for cp in hop(i, s - 1, d):
-                    cp.wait_recv()
-                val = val + dequantize(rq[i, s - 1], rs[i, s - 1])
-            quantize(val, sq.at[i, s], ss.at[i, s])
-            for cp in hop(i, s, d):
-                cp.start()
-        if s == 0:
-            for j in range(3, 8):
-                select(j)
-            products(3, 8)
-
+            remote(sq.at[g, i, s], rq.at[g, i, s], rq_s.at[g, i, s], rq_r.at[g, i, s], to),
+            remote(ss.at[g, i, s], rs.at[g, i, s], rs_s.at[g, i, s], rs_r.at[g, i, s], to),
+        )
+
+    def incoming(g, i, s, d):
+        for cp in hop(g, i, s, d):
+            cp.wait_recv()
+        return dequantize(rq[g, i, s], rs[g, i, s])
+
+    def advance(groups, s):
+        for g in groups:
+            for d, i, length in streams(g):
+                if s < length:
+                    val = chunk(d * (length - s), g)
+                    if s:
+                        val = val + incoming(g, i, s - 1, d)
+                    quantize(val, sq.at[g, i, s], ss.at[g, i, s])
+                    for cp in hop(g, i, s, d):
+                        cp.start()
+
+    o_mine = xor3(z, kappa)
+    end = jnp.where(z > o_mine, 1, 0)
+
+    def deliver(g, dc, mirror):
+        xx, cc = step(x, rel[g], 4), step(c, dc, 2)
+        lanes = pl.ds(pl.multiple_of(128 * cc, 128), 256)
+        slot = 2 * (z if mirror else o_mine) + end
+        n, m = g * 2 + dc, int(mirror)
+        to = dev(xx, y, cc, o_mine if mirror else z)
+        if not (g or dc or mirror):
+            return (
+                pltpu.make_async_copy(fq.at[g, :, lanes], gq.at[slot], own_s.at[2]),
+                pltpu.make_async_copy(fs.at[g], gs.at[slot], own_s.at[3]),
+            )
+        return (
+            remote(fq.at[g, :, lanes], gq.at[slot], fq_s.at[m, n], fq_r.at[m, kappa], to),
+            remote(fs.at[g], gs.at[slot], fs_s.at[m, n], fs_r.at[m, kappa], to),
+        )
+
+    def finish(groups):
+        for g in groups:
+            val = chunk(0, g)
+            for d, i, length in streams(g):
+                val = val + incoming(g, i, length - 1, d)
+            quantize(val, fq.at[g], fs.at[g])
+
+            @pl.when(kappa > 0)
+            def _():
+                for dc in (0, 1):
+                    for cp in deliver(g, dc, True):
+                        cp.start()
+
+            for dc in (0, 1):
+                for cp in deliver(g, dc, False):
+                    cp.start()
+
+    advance((0, 1), 0)
+    for j in (3, 4):
+        select(j)
+    products((0, 2), 3, 5)
+    advance((0, 1), 1)
+    for j in (5, 6, 7):
+        select(j)
+    products((0, 2), 5, 8)
+    other_core(1, -1)
+    other_core(3, 2)
+    products((2, 4), 0, 3)
+    advance((0, 1), 2)
+    advance((2, 3), 0)
+    products((2, 4), 3, 8)
+    advance((0, 1), 3)
+    advance((2, 3), 1)
     gq[2 * z + 1] = jnp.zeros(gq.shape[1:], gq.dtype)
     gs[2 * z + 1] = jnp.zeros(gs.shape[1:], gs.dtype)
-    for h in range(2):
-        val = chunk(0, h)
-        for i, (d, hh, length) in enumerate(streams):
-            if hh == h:
-                for cp in hop(i, length - 1, d):
-                    cp.wait_recv()
-                val = val + dequantize(rq[i, length - 1], rs[i, length - 1])
-        for i in range(2):
-            quantize(val[i : i + 1], fq.at[pl.ds(2 * h + i, 1)], fs.at[2 * h + i])
-
-    o = xor3(z, kappa)
-    end = jnp.where(z > o, 1, 0)
-
-    def deliver(dx, dc, mirror):
-        xx, cc = step(x, dx, 4), step(c, dc, 2)
-        lanes = pl.ds(pl.multiple_of(128 * cc, 128), 256)
-        slot = 2 * (z if mirror else o) + end
-        n, m = (dx * 2 + dc), int(mirror)
-        to = dev(xx, y, cc, o if mirror else z)
-        if not (dx or dc or mirror):
-            return (
-                pltpu.make_async_copy(fq.at[xx, :, lanes], gq.at[slot], own_s.at[2]),
-                pltpu.make_async_copy(fs.at[xx, :, lanes], gs.at[slot], own_s.at[3]),
-            )
-        return (
-            remote(fq.at[xx, :, lanes], gq.at[slot], fq_s.at[m, n], fq_r.at[m, kappa], to),
-            remote(fs.at[xx, :, lanes], gs.at[slot], fs_s.at[m, n], fs_r.at[m, kappa], to),
-        )
-
-    order = [(dx, dc) for dx in (2, 1, 3, 0) for dc in (0, 1)]
-
-    @pl.when(kappa > 0)
-    def _():
-        for dx, dc in order:
-            for cp in deliver(dx, dc, True):
-                cp.start()
-
-    for dx, dc in order:
-        for cp in deliver(dx, dc, False):
-            cp.start()
+    finish((0, 1))
+    advance((2, 3), 2)
+    advance((2, 3), 3)
+    finish((2, 3))
 
     def arrived(m, k):
         remote(fq.at[0, :, pl.ds(0, 256)], gq.at[0], fq_s.at[0, 0], fq_r.at[m, k], other).wait_recv()
-        remote(fs.at[0, :, pl.ds(0, 256)], gs.at[0], fs_s.at[0, 0], fs_r.at[m, k], other).wait_recv()
+        remote(fs.at[0], gs.at[0], fs_s.at[0, 0], fs_r.at[m, k], other).wait_recv()
 
     tn = (((0,), (0,)), ((), ()))
-    for n, (dx, dc) in enumerate(((0, 0), (0, 1), (1, 0), (1, 1), (3, 0), (3, 1), (2, 0), (2, 1))):
+    for n, (dx, dc) in enumerate(((0, 0), (0, 1), (3, 0), (3, 1), (1, 0), (1, 1), (2, 0), (2, 1))):
         k = kid(step(x, dx, 4), step(c, dc, 2))
         if dx or dc:
             arrived(0, k)
@@ -349,7 +389,7 @@
 
         o = xor3(z, k)
         full = jnp.concatenate(
-            [dequantize(gq[pl.ds(2 * o + i, 1)], gs[2 * o + i])[0] for i in range(2)], axis=0
+            [dequantize(gq[2 * o + i], gs[2 * o + i]) for i in range(2)], axis=0
         )
         top = full.astype(jnp.bfloat16)
         low = (full - top.astype(jnp.float32)).astype(jnp.bfloat16)
@@ -358,7 +398,12 @@
             low, w_rows, tn, preferred_element_type=jnp.float32
         )
         o_ref[...] = part if n == 0 else o_ref[...] + part
-    out_ref[...] = o_ref[pl.ds(pl.multiple_of(64 * c, 8), out_ref.shape[0]), :] / (ep_ref[...] - ev_ref[...])
+    leaving = []
+    for i in range(3):
+        rows = pl.ds(64 * i, 64)
+        out_ref[rows, :] = o_ref[pl.ds(pl.multiple_of(64 * (c + i), 8), 64), :] / (ep_ref[rows, :] - ev_ref[...])
+        leaving.append(pltpu.make_async_copy(out_ref.at[rows], out_hbm.at[rows], out_s.at[i]))
+        leaving[-1].start()
 
     for dx in range(4):
         for dc in range(2):
@@ -368,75 +413,78 @@
             for di in range(2):
                 remote(v_ref.at[0], v_buf.at[0, 0], vy_s.at[di, n], vx_r.at[0], other).wait_send()
             remote(v_ref.at[0], v_buf.at[0, 0], vf_s.at[n], vx_r.at[0], other).wait_send()
-    half_a = a_ref.at[pl.ds(0, 96)]
+    half_a = a_all.at[0, 0, pl.ds(0, 96)]
     for di in range(2):
         for h in range(2):
             remote(half_a, half_a, ax_s.at[di, h], ax_r.at[di, h], other).wait_send()
         remote(half_a, half_a, af_s.at[di], af_r.at[di], other).wait_send()
     for n in range(4):
         remote(a_ref, a_ref, ap_s.at[n], ap_r.at[n], other).wait_send()
-    for i, (d, h, length) in enumerate(streams):
-        for s in range(length):
-            for cp in hop(i, s, d):
-                cp.wait_send()
-    for dx, dc in order:
-        if dx or dc:
-            for cp in deliver(dx, dc, False):
-                cp.wait_send()
+    for g in range(4):
+        for d, i, length in streams(g):
+            for s in range(length):
+                for cp in hop(g, i, s, d):
+                    cp.wait_send()
+        for dc in (0, 1):
+            if g or dc:
+                for cp in deliver(g, dc, False):
+                    cp.wait_send()
 
     @pl.when(kappa > 0)
     def _():
-        for dx, dc in order:
-            for cp in deliver(dx, dc, True):
-                cp.wait_send()
+        for g in range(4):
+            for dc in (0, 1):
+                for cp in deliver(g, dc, True):
+                    cp.wait_send()
+
+    for cp in leaving:
+        cp.wait()
 
 
 def on_device(amplitudes, integrals, pair_index, eps_occ, eps_vir):
     rows, depth = amplitudes.shape
     f32, bf16, i16 = jnp.float32, jnp.bfloat16, jnp.int16
     dma = pltpu.SemaphoreType.DMA
+    sel, order = jnp.asarray(selection_tables(), bf16), jnp.asarray(row_order(), bf16)
+    table = jnp.asarray(output_tables())
+    vt, pairs, occ, vir = integrals.T, pair_index.T, eps_occ.reshape(1, -1), eps_vir.reshape(1, -1)
     return pl.pallas_call(
         kernel,
         out_shape=jax.ShapeDtypeStruct((rows, 8 * G * G), f32),
-        in_specs=[pl.BlockSpec(memory_space=pltpu.VMEM)] * 8,
-        out_specs=pl.BlockSpec(memory_space=pltpu.VMEM),
+        in_specs=[pl.BlockSpec(memory_space=pl.ANY)] * 8,
+        out_specs=pl.BlockSpec(memory_space=pl.ANY),
         scratch_shapes=[
+            *[pltpu.VMEM(a.shape, a.dtype) for a in (sel, order, table, vt, pairs, occ, vir)],
+            dma((8,)),
+            dma((3,)),
+            pltpu.VMEM((rows, 8 * G * G), f32),
             pltpu.VMEM((4, 2, rows, depth), bf16),
             pltpu.VMEM((8, ROWS, depth), bf16),
             pltpu.VMEM((8, 4, ROWS, depth), bf16),
             pltpu.VMEM((8 * HALF, depth), bf16),
             pltpu.VMEM((8 * HALF, depth), bf16),
             pltpu.VMEM((4, 8 * HALF, 2 * rows), f32),
-            pltpu.VMEM((4, 4, 2, HALF, 2 * rows), i16),
-            pltpu.VMEM((4, 4, 8, 2 * rows), bf16),
-            pltpu.VMEM((4, 4, 2, HALF, 2 * rows), i16),
-            pltpu.VMEM((4, 4, 8, 2 * rows), bf16),
+            pltpu.VMEM((4, 2, 4, HALF, 2 * rows), i16),
+            pltpu.VMEM((4, 2, 4, 8, 128), bf16),
+            pltpu.VMEM((4, 2, 4, HALF, 2 * rows), i16),
+            pltpu.VMEM((4, 2, 4, 8, 128), bf16),
             pltpu.VMEM((4, HALF, 2 * rows), i16),
-            pltpu.VMEM((4, 8, 2 * rows), bf16),
+            pltpu.VMEM((4, 8, 128), bf16),
             pltpu.VMEM((16, HALF, 256), i16),
-            pltpu.VMEM((16, 8, 256), bf16),
+            pltpu.VMEM((16, 8, 128), bf16),
             pltpu.VMEM((16 * HALF, 8 * G * G), bf16),
             pltpu.VMEM((256, 8 * G * G), f32),
             pltpu.VMEM((rows, 1), f32),
             pltpu.VMEM((1, 8 * G * G), f32),
             dma((8,)), dma((8,)), dma((2, 8)), dma((2, 8)), dma((8,)), dma((8,)),
             dma((2, 2)), dma((2, 2)), dma((2,)), dma((2,)), dma((4,)), dma((4,)), dma((4,)),
-            dma((4, 4)), dma((4, 4)), dma((4, 4)), dma((4, 4)),
+            dma((4, 2, 4)), dma((4, 2, 4)), dma((4, 2, 4)), dma((4, 2, 4)),
             dma((2, 8)), dma((2, 8)), dma((2, 8)), dma((2, 8)),
         ],
         compiler_params=pltpu.CompilerParams(
             collective_id=0, has_side_effects=True, vmem_limit_bytes=60 * 1024 * 1024
         ),
-    )(
-        jnp.asarray(selection_tables(), bf16),
-        jnp.asarray(row_order(), bf16),
-        jnp.asarray(output_tables()),
-        amplitudes,
-        integrals.T,
-        pair_index.T,
-        eps_occ.reshape(1, -1),
-        eps_vir.reshape(1, -1),
-    )
+    )(sel, order, table, amplitudes, vt, pairs, occ, vir)
 
 
 def solution(mesh):

time: 83.8 us -> 84.1 us (level)
  no operation moved by 1% of the time
where the time goes in v1:
time: 84.1 us; the launch traced here: 83.9 us
  Pallas kernels  81.8 us (97%)
  local copies, waits for them, and re-layouts  2.14 us (3%)
    pallas_call x1, Pallas kernels, on_device(): pl.pallas_call(kernel, out_shape=jax.ShapeDtypeStruct((rows, 8 * G * G),...  81.8 us
    unnamed x1, local copies, waits for them, and re-layouts  2.14 us

profile of v1, /device:TPU:1, one launch (start us, length us, event | category | flops | bytes accessed | tf_op | source)
XLA Modules:
  0.0 83.9 jit_solution(10230993263016268564)
XLA Ops:
  0.0 81.8 %shard_map.82 = f32[192,1152]{1,0:T(8,128)} custom-call(bf16[3,2,72,160]{3,2,1,0:T(8,128)(2,1)} %constant.6.clone.sel_hbm, bf16[320,288]{1,0:T(8,128)(2,1)} %constant.7.clone.order_hbm, s32[8,4,1152]{2,1,0:T(4,128)} %constant.8.clone.table_hbm, bf16[192,1152]{1,0:T(8,128)(2,1)} %a_hbm.1, bf16[288,1152]{1,0:T(8,128)(2,1)} %bitcast.4, s32[2,192]{1,0:T(2,128)} %bitcast.5, ...), custom_call_target="tpu_custom_call" | custom-call | tf_op jit(solution)/shard_map/pallas_call | solution.py:451
  81.8 2.1 %copy.10 = f32[192,1152]{1,0:T(8,128)} copy(f32[192,1152]{1,0:T(8,128)} %shard_map.82) | data formatting | bytes 1769472
